TPU v7x, 32 devices: a whole 2x2x4 slice. The times are simulated.
32 devices in a mesh: tm: 4 (over x, core), chan: 8 (over z, y).
Axes of the slice: x: 2, y: 2, z: 4, core: 2. Of those that a mesh axis runs over, the one named last changes fastest.
Arguments:
- samples: bfloat16 [384, 128], P('chan', 'tm'), may hold values from -6 to 6
- dead_channels: int32 [12], replicated, may hold values from 0 to 383
- first_kernel: bfloat16 [8, 32], replicated, may hold values from -3 to 3
- dilated_one: bfloat16 [3, 32, 64], replicated, may hold values from -0.875 to 0.875
- dilated_two: bfloat16 [3, 64, 128], replicated, may hold values from -0.625 to 0.625
- dilated_three: bfloat16 [3, 128, 256], replicated, may hold values from -0.4375 to 0.4375
- dilated_four: bfloat16 [3, 256, 256], replicated, may hold values from -0.3125 to 0.3125
- embed_weight: bfloat16 [256, 512], replicated, may hold values from -0.375 to 0.375
- gain_one: float32 [512], replicated, may hold values from 0.1 to 1.9
- project_in: bfloat16 [512, 1536], replicated, may hold values from -1 to 1
- project_out: bfloat16 [512, 512], replicated, may hold values from -0.25 to 0.25
- gain_two: float32 [512], replicated, may hold values from 0.1 to 1.9
- up_weight: bfloat16 [512, 2048], replicated, may hold values from -0.25 to 0.25
- down_weight: bfloat16 [2048, 512], replicated, may hold values from -0.125 to 0.125
Outputs:
- encoded: bfloat16 [32, 384, 512], P('tm', 'chan')
Inputs may be any that keep to these rules, and one draw needn't show every extreme that they name: `dead_channels`: channel numbers; a number may repeat.
All inputs are finite; a program needn't handle non-finite values.
Results may differ from a plain program's by a relative error of at most 0.015.
Values may be sent and summed in bfloat16 or wider, within the bound.
A program may use at most 64 MiB of HBM per device.

v0:
```python
import jax
import jax.numpy as jnp
from jax import lax
from jax.sharding import PartitionSpec as P

HEADS = 8
KERNEL = 8
STRIDE = 4


EPSILON = 1e-05
DILATIONS = (1, 2, 4, 8)


def extended_2(cells, sides, width):
    for axis, dim in sides:
        count = lax.axis_size(axis)
        ends = count - 1
        head = lax.slice_in_dim(cells, 0, width, axis=dim)
        tail = lax.slice_in_dim(cells, cells.shape[dim] - width, cells.shape[dim], axis=dim)
        cells = jnp.concatenate(
            [
                lax.ppermute(tail, axis, [(i, (i + 1) % count) for i in range(ends)]),
                cells,
                lax.ppermute(head, axis, [((i + 1) % count, i) for i in range(ends)]),
            ],
            axis=dim,
        )
    return cells


def normalize(tokens, gain):
    floats = tokens.astype(jnp.float32)
    average = jnp.mean(floats, axis=-1, keepdims=True)
    centred = floats - average
    variance = jnp.mean(centred * centred, axis=-1, keepdims=True)
    return (centred * lax.rsqrt(variance + EPSILON) * gain).astype(jnp.bfloat16)


def attend(query_rows, key_rows, value_rows, alive_mask):
    count = query_rows.shape[0]
    block_rows = min(512, count)
    scaling = query_rows.shape[2] ** (-0.5)

    def one_head(operands):
        queries, keys_head, values_head = operands
        blocks = queries.reshape(count // block_rows, block_rows, queries.shape[1])

        def one_block(query_block):
            scores = jnp.dot(query_block, keys_head.T, preferred_element_type=jnp.float32) * scaling
            scores = jnp.where(alive_mask[None, :], scores, -1e30)
            largest = jnp.max(scores, axis=1, keepdims=True)
            exponent = jnp.exp(scores - largest)
            weights = (exponent / jnp.sum(exponent, axis=1, keepdims=True)).astype(jnp.bfloat16)
            return jnp.dot(weights, values_head, preferred_element_type=jnp.float32).astype(
                jnp.bfloat16
            )

        return lax.map(one_block, blocks).reshape(count, queries.shape[1])

    heads_first = lax.map(
        one_head,
        (
            jnp.swapaxes(query_rows, 0, 1),
            jnp.swapaxes(key_rows, 0, 1),
            jnp.swapaxes(value_rows, 0, 1),
        ),
    )
    return jnp.swapaxes(heads_first, 0, 1).reshape(count, -1)


def encoder(
    embedded, alive_mask, gain_one, project_in, project_out, gain_two, up_weight, down_weight
):
    count, width = embedded.shape
    normed = normalize(embedded, gain_one)
    projected = jnp.dot(normed, project_in, preferred_element_type=jnp.float32).astype(jnp.bfloat16)
    pieces = projected.reshape(count, 3, HEADS, width // HEADS)
    attended = attend(pieces[:, 0], pieces[:, 1], pieces[:, 2], alive_mask)
    mixed = (
        embedded.astype(jnp.float32)
        + jnp.dot(attended, project_out, preferred_element_type=jnp.float32)
    ).astype(jnp.bfloat16)
    normed_two = normalize(mixed, gain_two)
    inner = jax.nn.gelu(jnp.dot(normed_two, up_weight, preferred_element_type=jnp.float32)).astype(
        jnp.bfloat16
    )
    return (
        mixed.astype(jnp.float32) + jnp.dot(inner, down_weight, preferred_element_type=jnp.float32)
    ).astype(jnp.bfloat16)


def patch_conv(padded, first_kernel, frames):
    taps = jnp.stack(
        [
            padded[:, offset : offset + STRIDE * (frames - 1) + 1 : STRIDE]
            for offset in range(KERNEL)
        ],
        axis=-1,
    )
    summed = jnp.einsum("cfk,ko->fco", taps, first_kernel, preferred_element_type=jnp.float32)
    return jax.nn.gelu(summed).astype(jnp.bfloat16)


def dilated(padded, weight, dilation, frames):
    summed = jnp.zeros((frames, padded.shape[1], weight.shape[2]), jnp.float32)
    for offset in range(3):
        window = padded[offset * dilation : offset * dilation + frames]
        summed = summed + jnp.einsum(
            "fci,io->fco", window, weight[offset], preferred_element_type=jnp.float32
        )
    return jax.nn.gelu(summed).astype(jnp.bfloat16)


def project_rows(features, embed_weight):
    return jnp.einsum(
        "fci,io->fco", features, embed_weight, preferred_element_type=jnp.float32
    ).astype(jnp.bfloat16)


def per_device(
    samples,
    dead_channels,
    first_kernel,
    dilated_one,
    dilated_two,
    dilated_three,
    dilated_four,
    embed_weight,
    gain_one,
    project_in,
    project_out,
    gain_two,
    up_weight,
    down_weight,
):
    channels_dev, sample_count = samples.shape
    groups = lax.axis_size("chan")
    channel_total = channels_dev * groups
    own_ids = lax.axis_index("chan") * channels_dev + jnp.arange(channels_dev, dtype=jnp.int32)
    own_alive = jnp.logical_not(jnp.any(own_ids[:, None] == dead_channels[None, :], axis=1))
    signal = jnp.where(own_alive[:, None], samples, jnp.zeros_like(samples))
    rim_width = (KERNEL - STRIDE) // 2
    weights_list = (dilated_one, dilated_two, dilated_three, dilated_four)
    padded = extended_2(signal, (("tm", 1),), rim_width)
    frames = sample_count // STRIDE
    hidden = patch_conv(padded, first_kernel, frames)
    for weight, dilation in zip(weights_list, DILATIONS):
        extended = extended_2(hidden, (("tm", 0),), dilation)
        hidden = dilated(extended, weight, dilation, frames)
    embedded = project_rows(hidden, embed_weight)
    embedded = lax.all_to_all(embedded, "chan", split_axis=0, concat_axis=1, tiled=True)
    all_ids = jnp.arange(channel_total, dtype=jnp.int32)
    alive_mask = jnp.logical_not(jnp.any(all_ids[:, None] == dead_channels[None, :], axis=1))

    def per_frame(frame_tokens):
        return encoder(
            frame_tokens,
            alive_mask,
            gain_one,
            project_in,
            project_out,
            gain_two,
            up_weight,
            down_weight,
        )

    result = lax.map(per_frame, embedded)
    return lax.all_to_all(result, "chan", split_axis=1, concat_axis=0, tiled=True)


def solution(mesh):
    return jax.shard_map(
        per_device,
        mesh=mesh,
        in_specs=(P("chan", "tm"), P(), P(), P(), P(), P(), P(), P(), P(), P(), P(), P(), P(), P()),
        out_specs=P("tm", "chan", None),
        check_vma=False,
    )
```

profile of v0, /device:TPU:0, one launch (start us, length us, event | category | flops | bytes accessed | tf_op | source)
XLA Modules:
  0.0 116.4 jit_solution(12862702731849805293)
XLA Ops:
  0.0 0.9 compare_reduce_fusion
  0.9 0.7 broadcast_select_fusion
  1.6 2.4 %collective-permute-start = (bf16[48,2]{0,1:T(2,128)(2,1)S(1)}, bf16[48,2]{0,1:T(2,128)(2,1)S(1)}, u32[]{:S(2)}, u32[]{:S(2)}) collective-permute-start(bf16[48,2]{0,1:T(2,128)(2,1)S(1)} %get-tuple-element.175), channel_id=1, source_target_pairs={{0,8},{8,16},{16,24},{1,9},{9,17},{17,25},{2,10},{10,18},{18,26},{... | collective-permute-start | bytes 584 | tf_op jit(solution)/shard_map/ppermute | solution.py:23
  4.0 1.3 %collective-permute-start.1 = (bf16[48,2]{0,1:T(2,128)(2,1)S(1)}, bf16[48,2]{0,1:T(2,128)(2,1)S(1)}, u32[]{:S(2)}, u32[]{:S(2)}) collective-permute-start(bf16[48,2]{0,1:T(2,128)(2,1)S(1)} %get-tuple-element.176), channel_id=1, source_target_pairs={{8,0},{16,8},{24,16},{9,1},{17,9},{25,17},{10,2},{18,10},{26,18},{... | collective-permute-start | bytes 584 | tf_op jit(solution)/shard_map/ppermute | solution.py:25
  5.5 3.7 %collective-permute-done.1 = bf16[48,2]{0,1:T(2,128)(2,1)S(1)} collective-permute-done((bf16[48,2]{0,1:T(2,128)(2,1)S(1)}, bf16[48,2]{0,1:T(2,128)(2,1)S(1)}, u32[]{:S(2)}, u32[]{:S(2)}) %collective-permute-start.1) | collective-permute-done | bytes 224 | tf_op jit(solution)/shard_map/ppermute | solution.py:25
  9.4 0.9 fusion.98
  10.3 1.3 %collective-permute-start.3 = (bf16[1,48,32]{1,2,0:T(8,128)(2,1)S(1)}, bf16[1,48,32]{1,2,0:T(8,128)(2,1)S(1)}, u32[]{:S(2)}, u32[]{:S(2)}) collective-permute-start(bf16[1,48,32]{1,2,0:T(8,128)(2,1)S(1)} %get-tuple-element.174), channel_id=1, source_target_pairs={{8,0},{16,8},{24,16},{9,1},{17,9},{25,17},{10,2},{18,10},{26,18},{... | collective-permute-start | bytes 9224 | tf_op jit(solution)/shard_map/ppermute | solution.py:25
  11.6 4.9 %collective-permute-start.2 = (bf16[1,48,32]{1,2,0:T(8,128)(2,1)S(1)}, bf16[1,48,32]{1,2,0:T(8,128)(2,1)S(1)}, u32[]{:S(2)}, u32[]{:S(2)}) collective-permute-start(bf16[1,48,32]{1,2,0:T(8,128)(2,1)S(1)} %get-tuple-element.173), channel_id=1, source_target_pairs={{0,8},{8,16},{16,24},{1,9},{9,17},{17,25},{2,10},{10,18},{18,26},{... | collective-permute-start | bytes 9224 | tf_op jit(solution)/shard_map/ppermute | solution.py:23
  16.5 0.9 fusion.139
  17.4 0.9 fusion.119
  18.3 1.0 fusion.71
  19.3 1.4 %collective-permute-start.5 = (bf16[2,48,64]{2,1,0:T(8,128)(2,1)S(1)}, bf16[2,48,64]{2,1,0:T(8,128)(2,1)S(1)}, u32[]{:S(2)}, u32[]{:S(2)}) collective-permute-start(bf16[2,48,64]{2,1,0:T(8,128)(2,1)S(1)} %get-tuple-element.172), channel_id=1, source_target_pairs={{8,0},{16,8},{24,16},{9,1},{17,9},{25,17},{10,2},{18,10},{26,18},{... | collective-permute-start | bytes 36872 | tf_op jit(solution)/shard_map/ppermute | solution.py:25
  20.7 0.9 fusion.132
  21.6 4.3 %collective-permute-start.4 = (bf16[2,48,64]{2,1,0:T(8,128)(2,1)S(1)}, bf16[2,48,64]{2,1,0:T(8,128)(2,1)S(1)}, u32[]{:S(2)}, u32[]{:S(2)}) collective-permute-start(bf16[2,48,64]{2,1,0:T(8,128)(2,1)S(1)} %get-tuple-element.171), channel_id=1, source_target_pairs={{0,8},{8,16},{16,24},{1,9},{9,17},{17,25},{2,10},{10,18},{18,26},{... | collective-permute-start | bytes 36872 | tf_op jit(solution)/shard_map/ppermute | solution.py:23
  25.9 0.1 fusion.112
  26.1 0.7 collective-permute-done.4
  26.7 0.2 fusion.79
  27.0 1.4 %collective-permute-start.7 = (bf16[4,48,128]{2,1,0:T(8,128)(2,1)S(1)}, bf16[4,48,128]{2,1,0:T(8,128)(2,1)S(1)}, u32[]{:S(2)}, u32[]{:S(2)}) collective-permute-start(bf16[4,48,128]{2,1,0:T(8,128)(2,1)S(1)} %get-tuple-element.170), channel_id=1, source_target_pairs={{8,0},{16,8},{24,16},{9,1},{17,9},{25,17},{10,2},{18,10},{26,18},{... | collective-permute-start | bytes 147464 | tf_op jit(solution)/shard_map/ppermute | solution.py:25
  28.4 0.2 fusion.124
  28.6 4.4 %collective-permute-start.6 = (bf16[4,48,128]{2,1,0:T(8,128)(2,1)S(1)}, bf16[4,48,128]{2,1,0:T(8,128)(2,1)S(1)}, u32[]{:S(2)}, u32[]{:S(2)}) collective-permute-start(bf16[4,48,128]{2,1,0:T(8,128)(2,1)S(1)} %get-tuple-element.169), channel_id=1, source_target_pairs={{0,8},{8,16},{16,24},{1,9},{9,17},{17,25},{2,10},{10,18},{18,26},{... | collective-permute-start | bytes 147464 | tf_op jit(solution)/shard_map/ppermute | solution.py:23
  33.0 0.2 fusion.87
  33.2 0.7 collective-permute-done.6
  33.8 0.3 fusion.47
  34.2 1.3 %collective-permute-start.9 = (bf16[8,48,256]{2,1,0:T(8,128)(2,1)S(1)}, bf16[8,48,256]{2,1,0:T(8,128)(2,1)S(1)}, u32[]{:S(2)}, u32[]{:S(2)}) collective-permute-start(bf16[8,48,256]{2,1,0:T(8,128)(2,1)S(1)} %fusion.47), channel_id=1, source_target_pairs={{8,0},{16,8},{24,16},{9,1},{17,9},{25,17},{10,2},{18,10},{26,18},{... | collective-permute-start | bytes 589832 | tf_op jit(solution)/shard_map/ppermute | solution.py:25
  35.5 5.8 %collective-permute-start.8 = (bf16[8,48,256]{2,1,0:T(8,128)(2,1)S(1)}, bf16[8,48,256]{2,1,0:T(8,128)(2,1)}, u32[]{:S(2)}, u32[]{:S(2)}) collective-permute-start(bf16[8,48,256]{2,1,0:T(8,128)(2,1)S(1)} %fusion.47), channel_id=1, source_target_pairs={{0,8},{8,16},{16,24},{1,9},{9,17},{17,25},{2,10},{10,18},{18,26},{... | collective-permute-start | bytes 589832 | tf_op jit(solution)/shard_map/ppermute | solution.py:23
  41.3 0.2 fusion.101
  41.5 0.2 fusion.99
  41.8 2.1 %convolution_convert_fusion.2 = bf16[8,48,512]{2,1,0:T(8,128)(2,1)} fusion(f32[8,48,256]{2,1,0:T(8,128)S(1)} %fusion.99, f32[8,48,256]{2,1,0:T(8,128)S(1)} %fusion.101, bf16[8,48,256]{2,1,0:T(8,128)(2,1)} %collective-permute-done.8, bf16[256,512]{1,0:T(8,128)(2,1)S(1)} %copy-done.5, bf16[3,256,256]{2,1,0:T(8,128)(2,1)S(1)} %copy-done.1), kind=kOutput, calls=%fused_computation.32 | convolution fusion | flops 152272896 | bytes 1769472 | tf_op jit(solution)/shard_map/fci,io->fco/dot_general | solution.py:116
  43.9 5.8 %all-to-all-start = ((bf16[8,48,512]{2,1,0:T(8,128)(2,1)}), bf16[8,48,512]{2,1,0:T(8,128)(2,1)S(1)}, u32[]{:S(2)}, u32[]{:S(2)}) async-start(bf16[8,48,512]{2,1,0:T(8,128)(2,1)} %convolution_convert_fusion.2), calls=%async_computation | async-start | bytes 786432 | tf_op jit(solution)/shard_map/all_to_all | solution.py:152
  49.9 9.2 %all-to-all-done = bf16[8,48,512]{2,1,0:T(8,128)(2,1)S(1)} async-done(((bf16[8,48,512]{2,1,0:T(8,128)(2,1)}), bf16[8,48,512]{2,1,0:T(8,128)(2,1)S(1)}, u32[]{:S(2)}, u32[]{:S(2)}) %all-to-all-start) | async-done | bytes 393248 | tf_op jit(solution)/shard_map/all_to_all | solution.py:152
  59.3 0.3 multiply_reduce_fusion.1
  59.6 0.2 fusion.39
  59.8 3.2 %convolution_convert_fusion.1 = bf16[384,1536]{1,0:T(8,128)(2,1)} fusion(bf16[384,512]{1,0:T(8,128)(2,1)S(1)} %fusion.39, bf16[512,1536]{1,0:T(8,128)(2,1)} %param.25), kind=kOutput, calls=%fused_computation.25 | convolution fusion | flops 604569600 | bytes 3145728 | tf_op jit(solution)/shard_map/while/body/eval_jaxpr/dot_general | solution.py:77
  63.1 2.4 %copy.148 = bf16[384,1536]{0,1:T(8,128)(2,1)} copy(bf16[384,1536]{1,0:T(8,128)(2,1)} %convolution_convert_fusion.1) | data formatting | bytes 2359296 | tf_op jit(solution)/shard_map/while/body/eval_jaxpr/convert_element_type | solution.py:77
  65.4 2.1 %slice_bitcast_fusion = (bf16[8,384,64]{1,2,0:T(8,128)(2,1)}, bf16[8,384,64]{1,2,0:T(8,128)(2,1)S(1)}, bf16[8,384,64]{1,2,0:T(8,128)(2,1)S(1)}) fusion(bf16[384,3,8,64]{0,3,2,1:T(8,128)(2,1)} %bitcast.143), kind=kLoop, calls=%fused_computation.70 | loop fusion | bytes 2359296 | tf_op jit(solution)/shard_map/while/body/eval_jaxpr/transpose | solution.py:66
  67.6 16.7 %while.17 = (s32[]{:T(128)}, bf16[8,384,64]{1,2,0:T(8,128)(2,1)}, pred[384]{0:T(512)(128)(4,1)S(1)}, bf16[8,384,64]{1,2,0:T(8,128)(2,1)S(1)}, bf16[8,384,64]{1,2...) while((s32[]{:T(128)}, bf16[8,384,64]{1,2,0:T(8,128)(2,1)}, pred[384]{0:T(512)(128)(4,1)S(1)}, ...), condition=%wide.region_7.8_spmd, body=%wide.region_4.7_spmd.sunk | while | flops 38952192 | bytes 1976397 | solution.py:61
  67.6 0.3 fusion.184
  67.9 0.1 fusion.185
  68.0 1.7 %fusion.186 = bf16[8,384,64]{1,2,0:T(8,128)(2,1)} fusion(bf16[8,384,64]{1,2,0:T(8,128)(2,1)} %get-tuple-element.228, s32[]{:T(128)} %get-tuple-element.227, f32[384,384]{0,1:T(8,128)S(1)} %get-tuple-element.218, f32[384]{0:T(512)S(1)} %fusion.185, f32[384]{0:T(512)S(1)} %get-tuple-element.219, bf16[8,384,64]{1,2,0:T(8,128)(2,1)} %get-tuple-element.239), kind=kOutput, calls=%fused_computation.4.clone.1 | convolution fusion | flops 19341312 | bytes 692224 | tf_op jit(solution)/shard_map/while/body/eval_jaxpr/while/body/eval_jaxpr/while/body/eval_jaxpr/dot_general | solution.py:55
  69.7 0.3 fusion.184
  70.0 0.1 fusion.185
  70.1 1.7 %fusion.186 = bf16[8,384,64]{1,2,0:T(8,128)(2,1)} fusion(bf16[8,384,64]{1,2,0:T(8,128)(2,1)} %get-tuple-element.228, s32[]{:T(128)} %get-tuple-element.227, f32[384,384]{0,1:T(8,128)S(1)} %get-tuple-element.218, f32[384]{0:T(512)S(1)} %fusion.185, f32[384]{0:T(512)S(1)} %get-tuple-element.219, bf16[8,384,64]{1,2,0:T(8,128)(2,1)} %get-tuple-element.239), kind=kOutput, calls=%fused_computation.4.clone.1 | convolution fusion | flops 19341312 | bytes 692224 | tf_op jit(solution)/shard_map/while/body/eval_jaxpr/while/body/eval_jaxpr/while/body/eval_jaxpr/dot_general | solution.py:55
  71.7 0.3 fusion.184
  72.2 1.7 %fusion.186 = bf16[8,384,64]{1,2,0:T(8,128)(2,1)} fusion(bf16[8,384,64]{1,2,0:T(8,128)(2,1)} %get-tuple-element.228, s32[]{:T(128)} %get-tuple-element.227, f32[384,384]{0,1:T(8,128)S(1)} %get-tuple-element.218, f32[384]{0:T(512)S(1)} %fusion.185, f32[384]{0:T(512)S(1)} %get-tuple-element.219, bf16[8,384,64]{1,2,0:T(8,128)(2,1)} %get-tuple-element.239), kind=kOutput, calls=%fused_computation.4.clone.1 | convolution fusion | flops 19341312 | bytes 692224 | tf_op jit(solution)/shard_map/while/body/eval_jaxpr/while/body/eval_jaxpr/while/body/eval_jaxpr/dot_general | solution.py:55
  73.8 0.3 fusion.184
  74.3 1.7 %fusion.186 = bf16[8,384,64]{1,2,0:T(8,128)(2,1)} fusion(bf16[8,384,64]{1,2,0:T(8,128)(2,1)} %get-tuple-element.228, s32[]{:T(128)} %get-tuple-element.227, f32[384,384]{0,1:T(8,128)S(1)} %get-tuple-element.218, f32[384]{0:T(512)S(1)} %fusion.185, f32[384]{0:T(512)S(1)} %get-tuple-element.219, bf16[8,384,64]{1,2,0:T(8,128)(2,1)} %get-tuple-element.239), kind=kOutput, calls=%fused_computation.4.clone.1 | convolution fusion | flops 19341312 | bytes 692224 | tf_op jit(solution)/shard_map/while/body/eval_jaxpr/while/body/eval_jaxpr/while/body/eval_jaxpr/dot_general | solution.py:55
  75.9 0.3 fusion.184
  76.3 1.7 %fusion.186 = bf16[8,384,64]{1,2,0:T(8,128)(2,1)} fusion(bf16[8,384,64]{1,2,0:T(8,128)(2,1)} %get-tuple-element.228, s32[]{:T(128)} %get-tuple-element.227, f32[384,384]{0,1:T(8,128)S(1)} %get-tuple-element.218, f32[384]{0:T(512)S(1)} %fusion.185, f32[384]{0:T(512)S(1)} %get-tuple-element.219, bf16[8,384,64]{1,2,0:T(8,128)(2,1)} %get-tuple-element.239), kind=kOutput, calls=%fused_computation.4.clone.1 | convolution fusion | flops 19341312 | bytes 692224 | tf_op jit(solution)/shard_map/while/body/eval_jaxpr/while/body/eval_jaxpr/while/body/eval_jaxpr/dot_general | solution.py:55
  78.0 0.3 fusion.184
  78.4 1.7 %fusion.186 = bf16[8,384,64]{1,2,0:T(8,128)(2,1)} fusion(bf16[8,384,64]{1,2,0:T(8,128)(2,1)} %get-tuple-element.228, s32[]{:T(128)} %get-tuple-element.227, f32[384,384]{0,1:T(8,128)S(1)} %get-tuple-element.218, f32[384]{0:T(512)S(1)} %fusion.185, f32[384]{0:T(512)S(1)} %get-tuple-element.219, bf16[8,384,64]{1,2,0:T(8,128)(2,1)} %get-tuple-element.239), kind=kOutput, calls=%fused_computation.4.clone.1 | convolution fusion | flops 19341312 | bytes 692224 | tf_op jit(solution)/shard_map/while/body/eval_jaxpr/while/body/eval_jaxpr/while/body/eval_jaxpr/dot_general | solution.py:55
  80.1 0.3 fusion.184
  80.5 1.7 %fusion.186 = bf16[8,384,64]{1,2,0:T(8,128)(2,1)} fusion(bf16[8,384,64]{1,2,0:T(8,128)(2,1)} %get-tuple-element.228, s32[]{:T(128)} %get-tuple-element.227, f32[384,384]{0,1:T(8,128)S(1)} %get-tuple-element.218, f32[384]{0:T(512)S(1)} %fusion.185, f32[384]{0:T(512)S(1)} %get-tuple-element.219, bf16[8,384,64]{1,2,0:T(8,128)(2,1)} %get-tuple-element.239), kind=kOutput, calls=%fused_computation.4.clone.1 | convolution fusion | flops 19341312 | bytes 692224 | tf_op jit(solution)/shard_map/while/body/eval_jaxpr/while/body/eval_jaxpr/while/body/eval_jaxpr/dot_general | solution.py:55
  82.2 0.3 fusion.184
  82.6 1.7 %fusion.186 = bf16[8,384,64]{1,2,0:T(8,128)(2,1)} fusion(bf16[8,384,64]{1,2,0:T(8,128)(2,1)} %get-tuple-element.228, s32[]{:T(128)} %get-tuple-element.227, f32[384,384]{0,1:T(8,128)S(1)} %get-tuple-element.218, f32[384]{0:T(512)S(1)} %fusion.185, f32[384]{0:T(512)S(1)} %get-tuple-element.219, bf16[8,384,64]{1,2,0:T(8,128)(2,1)} %get-tuple-element.239), kind=kOutput, calls=%fused_computation.4.clone.1 | convolution fusion | flops 19341312 | bytes 692224 | tf_op jit(solution)/shard_map/while/body/eval_jaxpr/while/body/eval_jaxpr/while/body/eval_jaxpr/dot_general | solution.py:55
  84.3 1.7 %fusion.165 = (f32[384]{0:T(512)S(1)}, f32[384,512]{1,0:T(8,128)S(1)}) fusion(bf16[384,512]{0,1:T(8,128)(2,1)} %bitcast.146, bf16[512,512]{1,0:T(8,128)(2,1)} %param.26, bf16[384,512]{1,0:T(8,128)(2,1)S(1)} %bitcast.142), kind=kOutput, calls=%fused_computation.188 | convolution fusion | flops 202309248 | bytes 2098688 | tf_op jit(solution)/shard_map/while/body/eval_jaxpr/dot_general | solution.py:82
  85.9 0.2 multiply_reduce_fusion
  86.2 4.4 %fusion.30 = bf16[1,384,512]{2,1,0:T(8,128)(2,1)} fusion(f32[384,512]{1,0:T(8,128)S(1)} %get-tuple-element.178, bf16[2048,512]{1,0:T(8,128)(2,1)S(1)} %copy-done, bf16[512,2048]{1,0:T(8,128)(2,1)} %param.28, f32[512]{0:T(512)S(1)} %copy-done.6, f32[384]{0:T(512)S(1)} %add_rsqrt_fusion.1, f32[384]{0:T(512)S(1)} %broadcast_multiply_fusion.1), kind=kOutput, calls=%fused_computation.33 | convolution fusion | flops 1618870272 | bytes 5379072 | tf_op jit(solution)/shard_map/while/body/eval_jaxpr/dot_general | solution.py:89
  90.6 1.6 %copy.158 = bf16[1,384,512]{2,0,1:T(2,128)(2,1)S(1)} copy(bf16[1,384,512]{2,1,0:T(8,128)(2,1)} %fusion.30) | data formatting | bytes 786432 | tf_op jit(solution)/shard_map/while/body/jit(dynamic_update_index_in_dim)/broadcast_in_dim | solution.py:168
  92.2 0.5 broadcast.175
  92.7 3.0 %reduce.8 = bf16[384,512]{1,0:T(8,128)(2,1)S(1)} reduce(bf16[384,1,512]{2,1,0:T(2,128)(2,1)S(1)} %bitcast.144, bf16[]{:T(256)} %broadcast.175), dimensions={1}, to_apply=%bitcast.133.reduce_sub_computation | reduce | bytes 786434
  95.8 0.3 reshape.104
  96.0 19.2 %all_to_all.21 = bf16[8,2,12288]{2,1,0:T(2,128)(2,1)S(1)} all-to-all(bf16[8,2,12288]{2,1,0:T(2,128)(2,1)S(1)} %reshape.104), channel_id=1, replica_groups=mesh['tm'=4,'chan'=8] {'chan'}, dimensions={0} | all-to-all | bytes 786432 | tf_op jit(solution)/shard_map/all_to_all | solution.py:169
  115.3 0.4 reshape.105
  115.6 0.8 copy.156
  (63 shorter events, 1.7 us)
Async XLA Ops:
  0.0 86.2 %copy-start = (bf16[2048,512]{1,0:T(8,128)(2,1)S(1)}, bf16[2048,512]{1,0:T(8,128)(2,1)}, u32[]{:S(2)}) copy-start(bf16[2048,512]{1,0:T(8,128)(2,1)} %param.29) | copy-start | bytes 6291460
  0.0 25.9 %copy-start.3 = (bf16[3,64,128]{2,1,0:T(8,128)(2,1)S(1)}, bf16[3,64,128]{2,1,0:T(8,128)(2,1)}, u32[]{:S(2)}) copy-start(bf16[3,64,128]{2,1,0:T(8,128)(2,1)} %param.20) | copy-start | bytes 147460
  0.0 28.4 %copy-start.2 = (bf16[3,128,256]{2,1,0:T(8,128)(2,1)S(1)}, bf16[3,128,256]{2,1,0:T(8,128)(2,1)}, u32[]{:S(2)}) copy-start(bf16[3,128,256]{2,1,0:T(8,128)(2,1)} %param.21) | copy-start | bytes 589828
  1.6 3.8 %collective-permute-start = (bf16[48,2]{0,1:T(2,128)(2,1)S(1)}, bf16[48,2]{0,1:T(2,128)(2,1)S(1)}, u32[]{:S(2)}, u32[]{:S(2)}) collective-permute-start(bf16[48,2]{0,1:T(2,128)(2,1)S(1)} %get-tuple-element.175), channel_id=1, source_target_pairs={{0,8},{8,16},{16,24},{1,9},{9,17},{17,25},{2,10},{10,18},{18,26},{... | collective-permute-start | bytes 584 | tf_op jit(solution)/shard_map/ppermute | solution.py:23
  4.0 5.1 %collective-permute-start.1 = (bf16[48,2]{0,1:T(2,128)(2,1)S(1)}, bf16[48,2]{0,1:T(2,128)(2,1)S(1)}, u32[]{:S(2)}, u32[]{:S(2)}) collective-permute-start(bf16[48,2]{0,1:T(2,128)(2,1)S(1)} %get-tuple-element.176), channel_id=1, source_target_pairs={{8,0},{16,8},{24,16},{9,1},{17,9},{25,17},{10,2},{18,10},{26,18},{... | collective-permute-start | bytes 584 | tf_op jit(solution)/shard_map/ppermute | solution.py:25
  10.3 7.1 %collective-permute-start.3 = (bf16[1,48,32]{1,2,0:T(8,128)(2,1)S(1)}, bf16[1,48,32]{1,2,0:T(8,128)(2,1)S(1)}, u32[]{:S(2)}, u32[]{:S(2)}) collective-permute-start(bf16[1,48,32]{1,2,0:T(8,128)(2,1)S(1)} %get-tuple-element.174), channel_id=1, source_target_pairs={{8,0},{16,8},{24,16},{9,1},{17,9},{25,17},{10,2},{18,10},{26,18},{... | collective-permute-start | bytes 9224 | tf_op jit(solution)/shard_map/ppermute | solution.py:25
  11.6 6.7 %collective-permute-start.2 = (bf16[1,48,32]{1,2,0:T(8,128)(2,1)S(1)}, bf16[1,48,32]{1,2,0:T(8,128)(2,1)S(1)}, u32[]{:S(2)}, u32[]{:S(2)}) collective-permute-start(bf16[1,48,32]{1,2,0:T(8,128)(2,1)S(1)} %get-tuple-element.173), channel_id=1, source_target_pairs={{0,8},{8,16},{16,24},{1,9},{9,17},{17,25},{2,10},{10,18},{18,26},{... | collective-permute-start | bytes 9224 | tf_op jit(solution)/shard_map/ppermute | solution.py:23
  19.3 22.0 %copy-start.1 = (bf16[3,256,256]{2,1,0:T(8,128)(2,1)S(1)}, bf16[3,256,256]{2,1,0:T(8,128)(2,1)}, u32[]{:S(2)}) copy-start(bf16[3,256,256]{2,1,0:T(8,128)(2,1)} %param.22) | copy-start | bytes 1179652
  19.3 6.6 %collective-permute-start.5 = (bf16[2,48,64]{2,1,0:T(8,128)(2,1)S(1)}, bf16[2,48,64]{2,1,0:T(8,128)(2,1)S(1)}, u32[]{:S(2)}, u32[]{:S(2)}) collective-permute-start(bf16[2,48,64]{2,1,0:T(8,128)(2,1)S(1)} %get-tuple-element.172), channel_id=1, source_target_pairs={{8,0},{16,8},{24,16},{9,1},{17,9},{25,17},{10,2},{18,10},{26,18},{... | collective-permute-start | bytes 36872 | tf_op jit(solution)/shard_map/ppermute | solution.py:25
  21.6 5.1 %collective-permute-start.4 = (bf16[2,48,64]{2,1,0:T(8,128)(2,1)S(1)}, bf16[2,48,64]{2,1,0:T(8,128)(2,1)S(1)}, u32[]{:S(2)}, u32[]{:S(2)}) collective-permute-start(bf16[2,48,64]{2,1,0:T(8,128)(2,1)S(1)} %get-tuple-element.171), channel_id=1, source_target_pairs={{0,8},{8,16},{16,24},{1,9},{9,17},{17,25},{2,10},{10,18},{18,26},{... | collective-permute-start | bytes 36872 | tf_op jit(solution)/shard_map/ppermute | solution.py:23
  26.9 14.9 %copy-start.5 = (bf16[256,512]{1,0:T(8,128)(2,1)S(1)}, bf16[256,512]{1,0:T(8,128)(2,1)}, u32[]{:S(2)}) copy-start(bf16[256,512]{1,0:T(8,128)(2,1)} %param.23) | copy-start | bytes 786436
  27.0 6.0 %collective-permute-start.7 = (bf16[4,48,128]{2,1,0:T(8,128)(2,1)S(1)}, bf16[4,48,128]{2,1,0:T(8,128)(2,1)S(1)}, u32[]{:S(2)}, u32[]{:S(2)}) collective-permute-start(bf16[4,48,128]{2,1,0:T(8,128)(2,1)S(1)} %get-tuple-element.170), channel_id=1, source_target_pairs={{8,0},{16,8},{24,16},{9,1},{17,9},{25,17},{10,2},{18,10},{26,18},{... | collective-permute-start | bytes 147464 | tf_op jit(solution)/shard_map/ppermute | solution.py:25
  28.6 5.2 %collective-permute-start.6 = (bf16[4,48,128]{2,1,0:T(8,128)(2,1)S(1)}, bf16[4,48,128]{2,1,0:T(8,128)(2,1)S(1)}, u32[]{:S(2)}, u32[]{:S(2)}) collective-permute-start(bf16[4,48,128]{2,1,0:T(8,128)(2,1)S(1)} %get-tuple-element.169), channel_id=1, source_target_pairs={{0,8},{8,16},{16,24},{1,9},{9,17},{17,25},{2,10},{10,18},{18,26},{... | collective-permute-start | bytes 147464 | tf_op jit(solution)/shard_map/ppermute | solution.py:23
  34.1 15.6 %copy-start.7 = (s32[12]{0:T(128)S(1)}, s32[12]{0:T(128)}, u32[]{:S(2)}) copy-start(s32[12]{0:T(128)} %param.17) | copy-start | bytes 148
  34.2 7.3 %collective-permute-start.9 = (bf16[8,48,256]{2,1,0:T(8,128)(2,1)S(1)}, bf16[8,48,256]{2,1,0:T(8,128)(2,1)S(1)}, u32[]{:S(2)}, u32[]{:S(2)}) collective-permute-start(bf16[8,48,256]{2,1,0:T(8,128)(2,1)S(1)} %fusion.47), channel_id=1, source_target_pairs={{8,0},{16,8},{24,16},{9,1},{17,9},{25,17},{10,2},{18,10},{26,18},{... | collective-permute-start | bytes 589832 | tf_op jit(solution)/shard_map/ppermute | solution.py:25
  35.5 6.3 %collective-permute-start.8 = (bf16[8,48,256]{2,1,0:T(8,128)(2,1)S(1)}, bf16[8,48,256]{2,1,0:T(8,128)(2,1)}, u32[]{:S(2)}, u32[]{:S(2)}) collective-permute-start(bf16[8,48,256]{2,1,0:T(8,128)(2,1)S(1)} %fusion.47), channel_id=1, source_target_pairs={{0,8},{8,16},{16,24},{1,9},{9,17},{17,25},{2,10},{10,18},{18,26},{... | collective-permute-start | bytes 589832 | tf_op jit(solution)/shard_map/ppermute | solution.py:23
  41.5 18.1 %copy-start.4 = (f32[512]{0:T(512)S(1)}, f32[512]{0:T(512)}, u32[]{:S(2)}) copy-start(f32[512]{0:T(512)} %param.24) | copy-start | bytes 6148
  43.9 15.1 %all-to-all-start = ((bf16[8,48,512]{2,1,0:T(8,128)(2,1)}), bf16[8,48,512]{2,1,0:T(8,128)(2,1)S(1)}, u32[]{:S(2)}, u32[]{:S(2)}) async-start(bf16[8,48,512]{2,1,0:T(8,128)(2,1)} %convolution_convert_fusion.2), calls=%async_computation | async-start | bytes 786432 | tf_op jit(solution)/shard_map/all_to_all | solution.py:152
  84.3 1.9 %copy-start.6 = (f32[512]{0:T(512)S(1)}, f32[512]{0:T(512)}, u32[]{:S(2)}) copy-start(f32[512]{0:T(512)} %param.27) | copy-start | bytes 6148
where the time goes:
time: 118 us; the launch traced here: 116 us
  starting transfers between devices  34.3 us (29%)
  matrix products  33.1 us (28%)
  blocking collectives  19.2 us (16%)
  waiting for transfers between devices  14.2 us (12%)
  local copies, waits for them, and re-layouts  8.62 us (7%)
  other arithmetic  6.6 us (6%)
    ppermute x5, starting transfers between devices, extended_2(): lax.ppermute(tail, axis, [(i, (i + 1) % count) for i in range(ends)])  21.7 us
    all_to_all x1, blocking collectives, per_device(): lax.all_to_all(result, 'chan', split_axis=1, concat_axis=0, tiled=True)  19.2 us
    dot_general x8, matrix products, one_block(): jnp.dot(weights, values_head, preferred_element_type=jnp.float32)  13.3 us
    all_to_all x1, waiting for transfers between devices, per_device(): lax.all_to_all(embedded, 'chan', split_axis=0, concat_axis=1, tiled=True)  9.17 us
    ppermute x5, starting transfers between devices, extended_2(): lax.ppermute(head, axis, [((i + 1) % count, i) for i in range(ends)])  6.72 us
    all_to_all x1, starting transfers between devices, per_device(): lax.all_to_all(embedded, 'chan', split_axis=0, concat_axis=1, tiled=True)  5.83 us
    dot_general x11, matrix products, dilated(): jnp.einsum('fci,io->fco', window, weight[offset], preferred_element_type=...  5.04 us
    dot_general x1, matrix products, encoder(): jnp.dot(inner, down_weight, preferred_element_type=jnp.float32)  4.41 us
  transfers between devices with their start and end apart: 11, of which 5 were waited for; matrix products, arithmetic and copies ran while one was open for 3% of the time, Pallas kernels for 0%

commit v1 on v0

v1 whole, which is shorter than its diff:
```python
import functools

import jax
import jax.numpy as jnp
from jax import lax
from jax.experimental import pallas as pl
from jax.experimental.pallas import tpu as pltpu
from jax.sharding import PartitionSpec as P

HEADS = 8
STRIDE = 4
EPSILON = 1e-05
REACH = 15
CONV_ROWS = 384
QUERY_ROWS = 192
MESH = pl.DeviceIdType.MESH


def gelu(v):
    half = 0.5 * v
    return half + half * jnp.tanh(v * (0.7978845608028654 + 0.035677408136300125 * (v * v)))


def dot(a, b):
    return jnp.dot(a, b, preferred_element_type=jnp.float32)


def normalize(tokens, gain):
    floats = tokens.astype(jnp.float32)
    centred = floats - jnp.mean(floats, axis=-1, keepdims=True)
    variance = jnp.mean(centred * centred, axis=-1, keepdims=True)
    return (centred * lax.rsqrt(variance + EPSILON) * gain).astype(jnp.bfloat16)


def looped(count, body):
    if count == 1:
        body(0)
    else:
        lax.fori_loop(0, count, lambda i, c: (body(i), c)[1], 0)


def kernel(
    groups_t,
    groups_c,
    dead,
    samples,
    first_kernel,
    one,
    two_hbm,
    three_hbm,
    four_hbm,
    embed_hbm,
    gain_one,
    pin_hbm,
    pout_hbm,
    gain_two,
    up_hbm,
    down_hbm,
    out,
    gathered,
    signal,
    toeplitz,
    one_wide,
    h0,
    h1,
    h2,
    h3,
    embedded,
    qkv,
    attended,
    result,
    two,
    three,
    four,
    embed,
    pin,
    pout,
    up,
    down,
    weight_sem,
    send_sem,
    recv_sem,
    out_send,
    out_recv,
    own_sem,
):
    devices = groups_t * groups_c
    my_t, my_c = lax.axis_index("tm"), lax.axis_index("chan")
    me = my_t * groups_c + my_c
    held, slab = samples.shape
    pack_rows = gathered.shape[1]
    packs = held // pack_rows
    total_samples = groups_t * slab
    frames = total_samples // STRIDE
    tokens = groups_c * held
    frame = my_t * (slab // STRIDE) + my_c

    barrier = pltpu.get_barrier_semaphore()

    def greet(i):
        peer = lax.rem(me + 1 + i, devices)
        pl.semaphore_signal(
            barrier, inc=1, device_id=(peer // groups_c, lax.rem(peer, groups_c)), device_id_type=MESH
        )

    looped(devices - 1, greet)

    loads = [
        pltpu.make_async_copy(src, dst, weight_sem.at[i])
        for i, (src, dst) in enumerate(
            [
                (two_hbm, two),
                (three_hbm, three),
                (four_hbm, four),
                (embed_hbm, embed),
                (pin_hbm, pin),
                (pout_hbm, pout),
                (up_hbm, up),
                (down_hbm, down),
            ]
        )
    ]
    for load in loads:
        load.start()

    row_ids = lax.broadcasted_iota(jnp.int32, (held, slab), 0) + my_c * held
    dead_rows = row_ids < 0
    for i in range(dead.shape[0]):
        dead_rows = jnp.logical_or(dead_rows, row_ids == dead[i])
    own = jnp.where(dead_rows, 0.0, samples[...].astype(jnp.float32)).astype(jnp.bfloat16)
    for a in range(packs):
        gathered[me, :, a * slab : (a + 1) * slab] = own[a * pack_rows : (a + 1) * pack_rows, :]

    pl.semaphore_wait(barrier, devices - 1)

    def spread(peer):
        return pltpu.make_async_remote_copy(
            src_ref=gathered.at[me],
            dst_ref=gathered.at[me],
            send_sem=send_sem.at[peer],
            recv_sem=recv_sem.at[me],
            device_id=(peer // groups_c, lax.rem(peer, groups_c)),
            device_id_type=MESH,
        )

    looped(devices - 1, lambda i: spread(lax.rem(me + 1 + i, devices)).start())

    c1 = first_kernel.shape[1]
    width = (2 * REACH + 2) * c1
    pick = lax.broadcasted_iota(jnp.int32, (c1, width), 0) == lax.rem(
        lax.broadcasted_iota(jnp.int32, (c1, width), 1), c1
    )
    tiled = dot(first_kernel[...], pick.astype(jnp.float32).astype(jnp.bfloat16))
    for start in range(0, total_samples, 128):
        size = min(128, total_samples - start)
        at_sample = lax.broadcasted_iota(jnp.int32, (size, width), 0) + start
        at_frame = lax.broadcasted_iota(jnp.int32, (size, width), 1) // c1 + (frame - REACH)
        tap = at_sample - STRIDE * at_frame + (first_kernel.shape[0] - STRIDE) // 2
        tap = jnp.where(jnp.logical_and(at_frame >= 0, at_frame < frames), tap, -1)
        band = jnp.zeros((size, width), jnp.float32)
        for k in range(first_kernel.shape[0]):
            band = jnp.where(tap == k, tiled[k : k + 1, :], band)
        toeplitz[start : start + size, :] = band.astype(jnp.bfloat16)
    c2 = one.shape[1]
    one_wide[...] = jnp.zeros_like(one_wide)
    one_wide[: 3 * c1, :c2] = one[...]
    one_wide[2 * c1 : 5 * c1, c2:] = one[...]

    key_ids = lax.broadcasted_iota(jnp.int32, (1, tokens), 1)
    dead_keys = key_ids < 0
    for i in range(dead.shape[0]):
        dead_keys = jnp.logical_or(dead_keys, key_ids == dead[i])
    key_bias = jnp.where(dead_keys, -1e30, 0.0)

    def arrived(i):
        peer = lax.rem(me + 1 + i, devices)
        pltpu.make_async_remote_copy(
            src_ref=gathered.at[peer],
            dst_ref=gathered.at[peer],
            send_sem=send_sem.at[peer],
            recv_sem=recv_sem.at[peer],
            device_id=(peer // groups_c, lax.rem(peer, groups_c)),
            device_id_type=MESH,
        ).wait_recv()

    looped(devices - 1, arrived)

    for t in range(groups_t):
        for a in range(packs):
            signal[:, a * pack_rows : (a + 1) * pack_rows, t * slab : (t + 1) * slab] = gathered[
                t * groups_c : (t + 1) * groups_c, :, a * slab : (a + 1) * slab
            ]

    def inside(offset):
        at = frame + offset
        return jnp.logical_and(at >= 0, at < frames).astype(jnp.float32)

    for load in loads[:5]:
        load.wait()

    def convolve(block):
        chans = CONV_ROWS // held
        rows = pl.ds(pl.multiple_of(block * CONV_ROWS, CONV_ROWS), CONV_ROWS)
        waves = signal[pl.ds(block * chans, chans)].reshape(CONV_ROWS, total_samples)
        for q in range(width // 256):
            cols = slice(q * 256, (q + 1) * 256)
            h0[:, cols] = gelu(dot(waves, toeplitz[:, cols])).astype(jnp.bfloat16)
        later = lax.broadcasted_iota(jnp.int32, (1, 2 * c2), 1) >= c2
        for q in range(8):
            depth = min(5 * c1, width - 128 * q)
            summed = gelu(dot(h0[:, 128 * q : 128 * q + depth], one_wide[:depth, :]))
            keep = jnp.where(later, inside(4 * q + 2 - 14), inside(4 * q - 14))
            h1[:, 128 * q : 128 * (q + 1)] = (summed * keep).astype(jnp.bfloat16)
        for n in range(7):
            summed = gelu(dot(h1[:, 128 * n : 128 * n + 192], two[...]))
            h2[:, 128 * n : 128 * (n + 1)] = (summed * inside(4 * n - 12)).astype(jnp.bfloat16)
        for p in range(3):
            summed = gelu(dot(h2[:, 256 * p : 256 * p + 384], three[...]))
            h3[:, 256 * p : 256 * (p + 1)] = (summed * inside(8 * p - 8)).astype(jnp.bfloat16)
        features = gelu(dot(h3[...], four[...])).astype(jnp.bfloat16)
        embedded_rows = dot(features, embed[...]).astype(jnp.bfloat16)
        embedded[rows, :] = embedded_rows
        normed = normalize(embedded_rows, gain_one[...])
        for q in range(pin.shape[1] // 256):
            cols = slice(q * 256, (q + 1) * 256)
            qkv[rows, cols] = dot(normed, pin[:, cols]).astype(jnp.bfloat16)

    looped(tokens // CONV_ROWS, convolve)

    for load in loads[5:]:
        load.wait()

    model = embed.shape[1]
    head = model // HEADS
    blocks = tokens // QUERY_ROWS
    peers = QUERY_ROWS // held
    my_block = my_c // peers

    def back(peer):
        return pltpu.make_async_remote_copy(
            src_ref=result.at[peer],
            dst_ref=out.at[my_c],
            send_sem=out_send.at[peer],
            recv_sem=out_recv.at[my_c],
            device_id=(my_t, peer),
            device_id_type=MESH,
        )

    keep_own = pltpu.make_async_copy(result.at[my_c], out.at[my_c], own_sem)

    def encode(step):
        block = lax.rem(my_block + 1 + step, blocks)
        rows = pl.ds(pl.multiple_of(block * QUERY_ROWS, QUERY_ROWS), QUERY_ROWS)
        low = lax.broadcasted_iota(jnp.int32, (1, 2 * head), 1) < head
        for pair in range(HEADS // 2):
            base = pair * 2 * head
            queries = qkv[rows, base : base + 2 * head].astype(jnp.float32) * (head**-0.5)
            keys = qkv[:, model + base : model + base + 2 * head]
            values = qkv[:, 2 * model + base : 2 * model + base + 2 * head]
            parts = []
            for mask in (low, jnp.logical_not(low)):
                masked = jnp.where(mask, queries, 0.0).astype(jnp.bfloat16)
                scores = lax.dot_general(
                    masked, keys, (((1,), (1,)), ((), ())), preferred_element_type=jnp.float32
                )
                scores = scores + key_bias
                exponent = jnp.exp(scores - jnp.max(scores, axis=1, keepdims=True))
                total = jnp.sum(exponent, axis=1, keepdims=True)
                parts.append(dot(exponent.astype(jnp.bfloat16), values) / total)
            attended[:, base : base + 2 * head] = jnp.where(low, parts[0], parts[1]).astype(jnp.bfloat16)
        mixed = (embedded[rows, :].astype(jnp.float32) + dot(attended[...], pout[...])).astype(jnp.bfloat16)
        normed = normalize(mixed, gain_two[...])
        total = mixed.astype(jnp.float32)
        for q in range(up.shape[1] // 512):
            cols = slice(q * 512, (q + 1) * 512)
            inner = gelu(dot(normed, up[:, cols])).astype(jnp.bfloat16)
            total = total + dot(inner, down[cols, :])
        result[pl.ds(block * peers, peers)] = total.astype(jnp.bfloat16).reshape(peers, held, model)
        for i in range(peers):
            peer = block * peers + i

            @pl.when(peer != my_c)
            def _():
                back(peer).start()

            @pl.when(peer == my_c)
            def _():
                keep_own.start()

    looped(blocks, encode)

    looped(devices - 1, lambda i: spread(lax.rem(me + 1 + i, devices)).wait_send())

    def finish(i):
        peer = lax.rem(my_c + 1 + i, groups_c)
        back(peer).wait_send()
        pltpu.make_async_remote_copy(
            src_ref=result.at[peer],
            dst_ref=out.at[peer],
            send_sem=out_send.at[peer],
            recv_sem=out_recv.at[peer],
            device_id=(my_t, peer),
            device_id_type=MESH,
        ).wait_recv()

    looped(groups_c - 1, finish)
    keep_own.wait()


def per_device(
    samples,
    dead_channels,
    first_kernel,
    dilated_one,
    dilated_two,
    dilated_three,
    dilated_four,
    embed_weight,
    gain_one,
    project_in,
    project_out,
    gain_two,
    up_weight,
    down_weight,
):
    groups_t, groups_c = lax.axis_size("tm"), lax.axis_size("chan")
    held, slab = samples.shape
    assert slab // STRIDE == groups_c
    devices = groups_t * groups_c
    tokens = groups_c * held
    packs = 3 if slab * 3 <= 128 and held % 48 == 0 else 1
    model = embed_weight.shape[1]
    flat = [w.reshape(w.shape[0] * w.shape[1], w.shape[2]) for w in (dilated_one, dilated_two, dilated_three, dilated_four)]
    bf16 = jnp.bfloat16
    width = (2 * REACH + 2) * first_kernel.shape[1]
    vmem = pl.BlockSpec(memory_space=pltpu.VMEM)
    anywhere = pl.BlockSpec(memory_space=pl.ANY)
    like = lambda w: pltpu.VMEM(w.shape, w.dtype)
    return pl.pallas_call(
        functools.partial(kernel, groups_t, groups_c),
        out_shape=jax.ShapeDtypeStruct((groups_c, held, model), bf16),
        in_specs=[pl.BlockSpec(memory_space=pltpu.SMEM), vmem, vmem, vmem]
        + [anywhere] * 4
        + [vmem, anywhere, anywhere, vmem, anywhere, anywhere],
        out_specs=anywhere,
        scratch_shapes=[
            pltpu.VMEM((devices, held // packs, 128 if packs > 1 else slab), bf16),
            pltpu.VMEM((groups_c, held, groups_t * slab), bf16),
            pltpu.VMEM((groups_t * slab, width), bf16),
            pltpu.VMEM((5 * dilated_one.shape[1], 2 * dilated_one.shape[2]), bf16),
            pltpu.VMEM((CONV_ROWS, width), bf16),
            pltpu.VMEM((CONV_ROWS, 8 * 128), bf16),
            pltpu.VMEM((CONV_ROWS, 7 * 128), bf16),
            pltpu.VMEM((CONV_ROWS, 3 * 256), bf16),
            pltpu.VMEM((tokens, model), bf16),
            pltpu.VMEM((tokens, 3 * model), bf16),
            pltpu.VMEM((QUERY_ROWS, model), bf16),
            pltpu.VMEM((groups_c, held, model), bf16),
        ]
        + [like(w) for w in flat[1:]]
        + [like(w) for w in (embed_weight, project_in, project_out, up_weight, down_weight)]
        + [
            pltpu.SemaphoreType.DMA((8,)),
            pltpu.SemaphoreType.DMA((devices,)),
            pltpu.SemaphoreType.DMA((devices,)),
            pltpu.SemaphoreType.DMA((groups_c,)),
            pltpu.SemaphoreType.DMA((groups_c,)),
            pltpu.SemaphoreType.DMA,
        ],
        compiler_params=pltpu.CompilerParams(
            collective_id=0, has_side_effects=True, vmem_limit_bytes=56 * 2**20
        ),
    )(
        dead_channels,
        samples,
        first_kernel,
        *flat,
        embed_weight,
        gain_one.reshape(1, -1),
        project_in,
        project_out,
        gain_two.reshape(1, -1),
        up_weight,
        down_weight,
    )


def solution(mesh):
    return jax.shard_map(
        per_device,
        mesh=mesh,
        in_specs=(P("chan", "tm"), P(), P(), P(), P(), P(), P(), P(), P(), P(), P(), P(), P(), P()),
        out_specs=P("tm", "chan", None),
        check_vma=False,
    )
```

time: 118 us -> 33.8 us (0.29); the launches traced: 116 us -> 33.5 us
  starting transfers between devices: 34.3 us -> 0 us
  matrix products: 33.1 us -> 0 us
  Pallas kernels: 0 us -> 30.4 us
  blocking collectives: 19.2 us -> 0 us
  waiting for transfers between devices: 14.2 us -> 0 us
  other arithmetic: 6.6 us -> 0 us
  local copies, waits for them, and re-layouts: 8.62 us -> 3.14 us
    dot_general x32 -> x0, matrix products: 33.1 us -> none  [the longest x8 13.3 us: one_block(): jnp.dot(weights, values_head, preferred_element_type=jnp.float32)]
    pallas_call x0 -> x1, Pallas kernels: none -> 30.4 us  [per_device(): pl.pallas_call(functools.partial(kernel, groups_t, groups_c), out_shape=j...]
    ppermute x10 -> x0, starting transfers between devices: 28.4 us -> none  [the longest x5 21.7 us: extended_2(): lax.ppermute(tail, axis, [(i, (i + 1) % count) for i in range(ends)])]
    all_to_all x1 -> x0, blocking collectives: 19.2 us -> none  [per_device(): lax.all_to_all(result, 'chan', split_axis=1, concat_axis=0, tiled=True)]
    all_to_all x1 -> x0, waiting for transfers between devices: 9.17 us -> none  [per_device(): lax.all_to_all(embedded, 'chan', split_axis=0, concat_axis=1, tiled=True)]
    all_to_all x1 -> x0, starting transfers between devices: 5.83 us -> none  [per_device(): lax.all_to_all(embedded, 'chan', split_axis=0, concat_axis=1, tiled=True)]
    ppermute x10 -> x0, waiting for transfers between devices: 5.08 us -> none  [the longest x5 3.67 us: extended_2(): lax.ppermute(head, axis, [((i + 1) % count, i) for i in range(ends)])]
    unnamed x1 -> x0, other arithmetic: 3.01 us -> none
  transfers between devices with their start and end apart: 11 -> 0, of which waited for: 5 -> 0; matrix products, arithmetic and copies ran while one was open for 3% -> 0% of each run, Pallas kernels for 0% -> 0%
where the time goes in v1:
time: 33.8 us; the launch traced here: 33.5 us
  Pallas kernels  30.4 us (90%)
  local copies, waits for them, and re-layouts  3.14 us (9%)
    pallas_call x1, Pallas kernels, per_device(): pl.pallas_call(functools.partial(kernel, groups_t, groups_c), out_shape=j...  30.4 us
    unnamed x2, local copies, waits for them, and re-layouts  3.14 us

profile of v1, /device:TPU:0, one launch (start us, length us, event | category | flops | bytes accessed | tf_op | source)
XLA Modules:
  0.0 33.5 jit_solution(9446167341291775096)
XLA Ops:
  0.0 1.4 %copy.15.samples = bf16[48,32]{1,0:T(8,128)(2,1)} copy(bf16[48,32]{0,1:T(8,128)(2,1)} %param.14) | data formatting | bytes 6144 | tf_op args[0]
  1.4 30.4 %shard_map.136 = bf16[8,48,512]{2,1,0:T(8,128)(2,1)} custom-call(s32[12]{0:T(128)} %dead.1, bf16[48,32]{1,0:T(8,128)(2,1)} %copy.15.samples, bf16[8,32]{1,0:T(8,128)(2,1)} %first_kernel.1, bf16[96,64]{1,0:T(8,128)(2,1)} %bitcast.9, bf16[192,128]{1,0:T(8,128)(2,1)} %bitcast.8, bf16[384,256]{1,0:T(8,128)(2,1)} %bitcast.7, bf16[768,256]{1,0:T(8,128)(2,1)} %bitcast.6, ...), custom_call_target="tpu_custom_call" | custom-call | tf_op jit(solution)/shard_map/pallas_call | solution.py:339
  31.8 1.8 %copy.17 = bf16[8,48,512]{2,1,0:T(8,128)(2,1)} copy(bf16[8,48,512]{2,1,0:T(8,128)(2,1)} %shard_map.136) | data formatting | bytes 786432

commit v2 on v1

--- a/solution.py
+++ b/solution.py
@@ -13,6 +13,7 @@
 REACH = 15
 CONV_ROWS = 384
 QUERY_ROWS = 192
+STACK = 4
 MESH = pl.DeviceIdType.MESH
 
 
@@ -80,14 +81,15 @@
     weight_sem,
     send_sem,
     recv_sem,
+    hand_send,
+    hand_recv,
     out_send,
     out_recv,
     own_sem,
 ):
-    devices = groups_t * groups_c
     my_t, my_c = lax.axis_index("tm"), lax.axis_index("chan")
     me = my_t * groups_c + my_c
-    held, slab = samples.shape
+    slab, held = samples.shape
     pack_rows = gathered.shape[1]
     packs = held // pack_rows
     total_samples = groups_t * slab
@@ -97,13 +99,16 @@
 
     barrier = pltpu.get_barrier_semaphore()
 
-    def greet(i):
-        peer = lax.rem(me + 1 + i, devices)
-        pl.semaphore_signal(
-            barrier, inc=1, device_id=(peer // groups_c, lax.rem(peer, groups_c)), device_id_type=MESH
-        )
-
-    looped(devices - 1, greet)
+    def greet_chan(i):
+        peer = lax.rem(my_c + 1 + i, groups_c)
+        pl.semaphore_signal(barrier, inc=1, device_id=(my_t, peer), device_id_type=MESH)
+
+    def greet_time(i):
+        peer = lax.rem(my_t + 1 + i, groups_t)
+        pl.semaphore_signal(barrier, inc=1, device_id=(peer, my_c), device_id_type=MESH)
+
+    looped(groups_c - 1, greet_chan)
+    looped(groups_t - 1, greet_time)
 
     loads = [
         pltpu.make_async_copy(src, dst, weight_sem.at[i])
@@ -123,27 +128,50 @@
     for load in loads:
         load.start()
 
-    row_ids = lax.broadcasted_iota(jnp.int32, (held, slab), 0) + my_c * held
-    dead_rows = row_ids < 0
+    row_ids = lax.broadcasted_iota(jnp.int32, (held, held), 0)
+    alive = row_ids == lax.broadcasted_iota(jnp.int32, (held, held), 1)
+    row_ids = row_ids + my_c * held
     for i in range(dead.shape[0]):
-        dead_rows = jnp.logical_or(dead_rows, row_ids == dead[i])
-    own = jnp.where(dead_rows, 0.0, samples[...].astype(jnp.float32)).astype(jnp.bfloat16)
+        alive = jnp.logical_and(alive, row_ids != dead[i])
+    own = lax.dot_general(
+        jnp.where(alive, 1.0, 0.0).astype(jnp.bfloat16),
+        samples[...],
+        (((1,), (1,)), ((), ())),
+        preferred_element_type=jnp.float32,
+    ).astype(jnp.bfloat16)
     for a in range(packs):
         gathered[me, :, a * slab : (a + 1) * slab] = own[a * pack_rows : (a + 1) * pack_rows, :]
 
-    pl.semaphore_wait(barrier, devices - 1)
-
-    def spread(peer):
+    pl.semaphore_wait(barrier, groups_c + groups_t - 2)
+
+    def spread(peer, slot):
         return pltpu.make_async_remote_copy(
-            src_ref=gathered.at[me],
-            dst_ref=gathered.at[me],
+            src_ref=gathered.at[my_t * groups_c + slot],
+            dst_ref=gathered.at[my_t * groups_c + slot],
             send_sem=send_sem.at[peer],
-            recv_sem=recv_sem.at[me],
-            device_id=(peer // groups_c, lax.rem(peer, groups_c)),
+            recv_sem=recv_sem.at[slot],
+            device_id=(my_t, peer),
             device_id_type=MESH,
         )
 
-    looped(devices - 1, lambda i: spread(lax.rem(me + 1 + i, devices)).start())
+    def hand(peer, slab_at):
+        slots = pl.ds(slab_at * groups_c, groups_c)
+        return pltpu.make_async_remote_copy(
+            src_ref=gathered.at[slots],
+            dst_ref=gathered.at[slots],
+            send_sem=hand_send.at[peer],
+            recv_sem=hand_recv.at[slab_at],
+            device_id=(peer, my_c),
+            device_id_type=MESH,
+        )
+
+    def chan_peer(i):
+        return lax.rem(my_c + 1 + i, groups_c)
+
+    def time_peer(i):
+        return lax.rem(my_t + 1 + i, groups_t)
+
+    looped(groups_c - 1, lambda i: spread(chan_peer(i), my_c).start())
 
     c1 = first_kernel.shape[1]
     width = (2 * REACH + 2) * c1
@@ -151,6 +179,20 @@
         lax.broadcasted_iota(jnp.int32, (c1, width), 1), c1
     )
     tiled = dot(first_kernel[...], pick.astype(jnp.float32).astype(jnp.bfloat16))
+    c2 = one.shape[1]
+    one_wide[...] = jnp.zeros_like(one_wide)
+    one_wide[: 3 * c1, :c2] = one[...]
+    one_wide[2 * c1 : 5 * c1, c2:] = one[...]
+
+    key_ids = lax.broadcasted_iota(jnp.int32, (1, tokens), 1)
+    dead_keys = key_ids < 0
+    for i in range(dead.shape[0]):
+        dead_keys = jnp.logical_or(dead_keys, key_ids == dead[i])
+    key_bias = jnp.where(dead_keys, -1e30, 0.0)
+
+    looped(groups_c - 1, lambda i: spread(chan_peer(i), chan_peer(i)).wait_recv())
+    looped(groups_t - 1, lambda i: hand(time_peer(i), my_t).start())
+
     for start in range(0, total_samples, 128):
         size = min(128, total_samples - start)
         at_sample = lax.broadcasted_iota(jnp.int32, (size, width), 0) + start
@@ -161,29 +203,8 @@
         for k in range(first_kernel.shape[0]):
             band = jnp.where(tap == k, tiled[k : k + 1, :], band)
         toeplitz[start : start + size, :] = band.astype(jnp.bfloat16)
-    c2 = one.shape[1]
-    one_wide[...] = jnp.zeros_like(one_wide)
-    one_wide[: 3 * c1, :c2] = one[...]
-    one_wide[2 * c1 : 5 * c1, c2:] = one[...]
-
-    key_ids = lax.broadcasted_iota(jnp.int32, (1, tokens), 1)
-    dead_keys = key_ids < 0
-    for i in range(dead.shape[0]):
-        dead_keys = jnp.logical_or(dead_keys, key_ids == dead[i])
-    key_bias = jnp.where(dead_keys, -1e30, 0.0)
-
-    def arrived(i):
-        peer = lax.rem(me + 1 + i, devices)
-        pltpu.make_async_remote_copy(
-            src_ref=gathered.at[peer],
-            dst_ref=gathered.at[peer],
-            send_sem=send_sem.at[peer],
-            recv_sem=recv_sem.at[peer],
-            device_id=(peer // groups_c, lax.rem(peer, groups_c)),
-            device_id_type=MESH,
-        ).wait_recv()
-
-    looped(devices - 1, arrived)
+
+    looped(groups_t - 1, lambda i: hand(time_peer(i), time_peer(i)).wait_recv())
 
     for t in range(groups_t):
         for a in range(packs):
@@ -249,25 +270,31 @@
     keep_own = pltpu.make_async_copy(result.at[my_c], out.at[my_c], own_sem)
 
     def encode(step):
-        block = lax.rem(my_block + 1 + step, blocks)
+        half = blocks // 2
+        far = 1 - step // half
+        side = lax.rem(my_block // half + far, 2)
+        block = side * half + lax.rem(my_block + 1 + step, half)
         rows = pl.ds(pl.multiple_of(block * QUERY_ROWS, QUERY_ROWS), QUERY_ROWS)
-        low = lax.broadcasted_iota(jnp.int32, (1, 2 * head), 1) < head
-        for pair in range(HEADS // 2):
-            base = pair * 2 * head
-            queries = qkv[rows, base : base + 2 * head].astype(jnp.float32) * (head**-0.5)
-            keys = qkv[:, model + base : model + base + 2 * head]
-            values = qkv[:, 2 * model + base : 2 * model + base + 2 * head]
-            parts = []
-            for mask in (low, jnp.logical_not(low)):
-                masked = jnp.where(mask, queries, 0.0).astype(jnp.bfloat16)
-                scores = lax.dot_general(
-                    masked, keys, (((1,), (1,)), ((), ())), preferred_element_type=jnp.float32
-                )
-                scores = scores + key_bias
-                exponent = jnp.exp(scores - jnp.max(scores, axis=1, keepdims=True))
-                total = jnp.sum(exponent, axis=1, keepdims=True)
-                parts.append(dot(exponent.astype(jnp.bfloat16), values) / total)
-            attended[:, base : base + 2 * head] = jnp.where(low, parts[0], parts[1]).astype(jnp.bfloat16)
+        span = STACK * head
+        lane_head = lax.broadcasted_iota(jnp.int32, (1, span), 1) // head
+        for base in range(0, model, span):
+            queries = qkv[rows, base : base + span].astype(jnp.float32) * (head**-0.5)
+            keys = qkv[:, model + base : model + base + span]
+            values = qkv[:, 2 * model + base : 2 * model + base + span]
+            stacked = jnp.concatenate(
+                [jnp.where(lane_head == h, queries, 0.0).astype(jnp.bfloat16) for h in range(STACK)], axis=0
+            )
+            scores = lax.dot_general(
+                stacked, keys, (((1,), (1,)), ((), ())), preferred_element_type=jnp.float32
+            )
+            scores = scores + key_bias
+            exponent = jnp.exp(scores - jnp.max(scores, axis=1, keepdims=True))
+            total = jnp.sum(exponent, axis=1, keepdims=True)
+            mean = dot(exponent.astype(jnp.bfloat16), values) / total
+            merged = mean[:QUERY_ROWS]
+            for h in range(1, STACK):
+                merged = jnp.where(lane_head == h, mean[h * QUERY_ROWS : (h + 1) * QUERY_ROWS], merged)
+            attended[:, base : base + span] = merged.astype(jnp.bfloat16)
         mixed = (embedded[rows, :].astype(jnp.float32) + dot(attended[...], pout[...])).astype(jnp.bfloat16)
         normed = normalize(mixed, gain_two[...])
         total = mixed.astype(jnp.float32)
@@ -289,7 +316,8 @@
 
     looped(blocks, encode)
 
-    looped(devices - 1, lambda i: spread(lax.rem(me + 1 + i, devices)).wait_send())
+    looped(groups_c - 1, lambda i: spread(chan_peer(i), my_c).wait_send())
+    looped(groups_t - 1, lambda i: hand(time_peer(i), my_t).wait_send())
 
     def finish(i):
         peer = lax.rem(my_c + 1 + i, groups_c)
@@ -361,8 +389,10 @@
         + [like(w) for w in (embed_weight, project_in, project_out, up_weight, down_weight)]
         + [
             pltpu.SemaphoreType.DMA((8,)),
-            pltpu.SemaphoreType.DMA((devices,)),
-            pltpu.SemaphoreType.DMA((devices,)),
+            pltpu.SemaphoreType.DMA((groups_c,)),
+            pltpu.SemaphoreType.DMA((groups_c,)),
+            pltpu.SemaphoreType.DMA((groups_t,)),
+            pltpu.SemaphoreType.DMA((groups_t,)),
             pltpu.SemaphoreType.DMA((groups_c,)),
             pltpu.SemaphoreType.DMA((groups_c,)),
             pltpu.SemaphoreType.DMA,
@@ -372,7 +402,7 @@
         ),
     )(
         dead_channels,
-        samples,
+        samples.T,
         first_kernel,
         *flat,
         embed_weight,

time: 33.8 us -> 31.9 us (0.944)
  local copies, waits for them, and re-layouts: 3.14 us -> 1.77 us
  Pallas kernels: 30.4 us -> 29.9 us
    unnamed x2 -> x1, local copies, waits for them, and re-layouts: 3.14 us -> 1.77 us
    pallas_call x1, Pallas kernels: 30.4 us -> 29.9 us  [per_device(): pl.pallas_call(functools.partial(kernel, groups_t, groups_c), out_shape=j...]
where the time goes in v2:
time: 31.9 us; the launch traced here: 31.6 us
  Pallas kernels  29.9 us (94%)
  local copies, waits for them, and re-layouts  1.77 us (6%)
    pallas_call x1, Pallas kernels, per_device(): pl.pallas_call(functools.partial(kernel, groups_t, groups_c), out_shape=j...  29.9 us
    unnamed x1, local copies, waits for them, and re-layouts  1.77 us

profile of v2, /device:TPU:0, one launch (start us, length us, event | category | flops | bytes accessed | tf_op | source)
XLA Modules:
  0.0 31.6 jit_solution(15209836026739916786)
XLA Ops:
  0.0 29.9 %shard_map.136 = bf16[8,48,512]{2,1,0:T(8,128)(2,1)} custom-call(s32[12]{0:T(128)} %dead.1, bf16[32,48]{1,0:T(8,128)(2,1)} %bitcast.11, bf16[8,32]{1,0:T(8,128)(2,1)} %first_kernel.1, bf16[96,64]{1,0:T(8,128)(2,1)} %bitcast.10, bf16[192,128]{1,0:T(8,128)(2,1)} %bitcast.9, bf16[384,256]{1,0:T(8,128)(2,1)} %bitcast.8, bf16[768,256]{1,0:T(8,128)(2,1)} %bitcast.7, ...), custom_call_target="tpu_custom_call" | custom-call | tf_op jit(solution)/shard_map/pallas_call | solution.py:367
  29.9 1.8 %copy.16 = bf16[8,48,512]{2,1,0:T(8,128)(2,1)} copy(bf16[8,48,512]{2,1,0:T(8,128)(2,1)} %shard_map.136) | data formatting | bytes 786432

commit v3 on v2

--- a/solution.py
+++ b/solution.py
@@ -31,6 +31,10 @@
     centred = floats - jnp.mean(floats, axis=-1, keepdims=True)
     variance = jnp.mean(centred * centred, axis=-1, keepdims=True)
     return (centred * lax.rsqrt(variance + EPSILON) * gain).astype(jnp.bfloat16)
+
+
+def third_offsets(gap):
+    return sorted({part * gap + 8 * k for part in range(2) for k in (-1, 0, 1)})
 
 
 def looped(count, body):
@@ -67,7 +71,8 @@
     h2,
     h3,
     embedded,
-    qkv,
+    normed_all,
+    kv,
     attended,
     result,
     two,
@@ -95,7 +100,9 @@
     total_samples = groups_t * slab
     frames = total_samples // STRIDE
     tokens = groups_c * held
-    frame = my_t * (slab // STRIDE) + my_c
+    gap = groups_c // 2
+    my_side, my_lane = my_c // gap, lax.rem(my_c, gap)
+    frame = my_t * (slab // STRIDE) + my_lane
 
     barrier = pltpu.get_barrier_semaphore()
 
@@ -174,7 +181,7 @@
     looped(groups_c - 1, lambda i: spread(chan_peer(i), my_c).start())
 
     c1 = first_kernel.shape[1]
-    width = (2 * REACH + 2) * c1
+    width = toeplitz.shape[1]
     pick = lax.broadcasted_iota(jnp.int32, (c1, width), 0) == lax.rem(
         lax.broadcasted_iota(jnp.int32, (c1, width), 1), c1
     )
@@ -219,68 +226,80 @@
     for load in loads[:5]:
         load.wait()
 
+    model = embed.shape[1]
+    head = model // HEADS
+
     def convolve(block):
         chans = CONV_ROWS // held
         rows = pl.ds(pl.multiple_of(block * CONV_ROWS, CONV_ROWS), CONV_ROWS)
         waves = signal[pl.ds(block * chans, chans)].reshape(CONV_ROWS, total_samples)
-        for q in range(width // 256):
-            cols = slice(q * 256, (q + 1) * 256)
+        for start in range(0, width, 256):
+            cols = slice(start, min(start + 256, width))
             h0[:, cols] = gelu(dot(waves, toeplitz[:, cols])).astype(jnp.bfloat16)
         later = lax.broadcasted_iota(jnp.int32, (1, 2 * c2), 1) >= c2
-        for q in range(8):
+        for q in range(h1.shape[1] // 128):
             depth = min(5 * c1, width - 128 * q)
             summed = gelu(dot(h0[:, 128 * q : 128 * q + depth], one_wide[:depth, :]))
             keep = jnp.where(later, inside(4 * q + 2 - 14), inside(4 * q - 14))
             h1[:, 128 * q : 128 * (q + 1)] = (summed * keep).astype(jnp.bfloat16)
-        for n in range(7):
+        for n in range(h2.shape[1] // 128):
             summed = gelu(dot(h1[:, 128 * n : 128 * n + 192], two[...]))
             h2[:, 128 * n : 128 * (n + 1)] = (summed * inside(4 * n - 12)).astype(jnp.bfloat16)
-        for p in range(3):
-            summed = gelu(dot(h2[:, 256 * p : 256 * p + 384], three[...]))
-            h3[:, 256 * p : 256 * (p + 1)] = (summed * inside(8 * p - 8)).astype(jnp.bfloat16)
-        features = gelu(dot(h3[...], four[...])).astype(jnp.bfloat16)
-        embedded_rows = dot(features, embed[...]).astype(jnp.bfloat16)
-        embedded[rows, :] = embedded_rows
-        normed = normalize(embedded_rows, gain_one[...])
-        for q in range(pin.shape[1] // 256):
-            cols = slice(q * 256, (q + 1) * 256)
-            qkv[rows, cols] = dot(normed, pin[:, cols]).astype(jnp.bfloat16)
+        thirds = third_offsets(gap)
+        for p, offset in enumerate(thirds):
+            n = (offset + 8) // 4
+            summed = gelu(dot(h2[:, 128 * n : 128 * n + 384], three[...]))
+            h3[:, 256 * p : 256 * (p + 1)] = (summed * inside(offset)).astype(jnp.bfloat16)
+        for part in range(2):
+            summed = None
+            for k in range(3):
+                p = thirds.index(part * gap + 8 * (k - 1))
+                term = dot(h3[:, 256 * p : 256 * (p + 1)], four[256 * k : 256 * (k + 1), :])
+                summed = term if summed is None else summed + term
+            embedded_rows = dot(gelu(summed).astype(jnp.bfloat16), embed[...]).astype(jnp.bfloat16)
+            embedded[part, rows, :] = embedded_rows
+            normed = normalize(embedded_rows, gain_one[...])
+            normed_all[part, rows, :] = normed
+            for q in range(kv.shape[2] // 256):
+                cols = slice(q * 256, (q + 1) * 256)
+                kv[part, rows, cols] = dot(
+                    normed, pin[:, model + q * 256 : model + (q + 1) * 256]
+                ).astype(jnp.bfloat16)
 
     looped(tokens // CONV_ROWS, convolve)
 
     for load in loads[5:]:
         load.wait()
 
-    model = embed.shape[1]
-    head = model // HEADS
     blocks = tokens // QUERY_ROWS
     peers = QUERY_ROWS // held
-    my_block = my_c // peers
-
-    def back(peer):
+
+    def back(part, peer):
         return pltpu.make_async_remote_copy(
-            src_ref=result.at[peer],
-            dst_ref=out.at[my_c],
-            send_sem=out_send.at[peer],
-            recv_sem=out_recv.at[my_c],
-            device_id=(my_t, peer),
+            src_ref=result.at[part * gap + peer],
+            dst_ref=out.at[part * gap + my_lane],
+            send_sem=out_send.at[part * gap + peer],
+            recv_sem=out_recv.at[part * gap + my_lane],
+            device_id=(my_t, my_side * gap + peer),
             device_id_type=MESH,
         )
 
-    keep_own = pltpu.make_async_copy(result.at[my_c], out.at[my_c], own_sem)
+    def keep_own(part):
+        at = part * gap + my_lane
+        return pltpu.make_async_copy(result.at[at], out.at[at], own_sem.at[part])
 
     def encode(step):
-        half = blocks // 2
-        far = 1 - step // half
-        side = lax.rem(my_block // half + far, 2)
-        block = side * half + lax.rem(my_block + 1 + step, half)
-        rows = pl.ds(pl.multiple_of(block * QUERY_ROWS, QUERY_ROWS), QUERY_ROWS)
+        part = step // (blocks // 2)
+        block = lax.rem(step, blocks // 2)
+        start = my_side * (tokens // 2) + block * QUERY_ROWS
+        rows = pl.ds(pl.multiple_of(start, QUERY_ROWS), QUERY_ROWS)
+        all_queries = dot(normed_all[part, rows, :], pin[:, :model]).astype(jnp.bfloat16)
         span = STACK * head
         lane_head = lax.broadcasted_iota(jnp.int32, (1, span), 1) // head
         for base in range(0, model, span):
-            queries = qkv[rows, base : base + span].astype(jnp.float32) * (head**-0.5)
-            keys = qkv[:, model + base : model + base + span]
-            values = qkv[:, 2 * model + base : 2 * model + base + span]
+            queries = all_queries[:, base : base + span].astype(jnp.float32) * (head**-0.5)
+            keys = kv[part, :, base : base + span]
+            values = kv[part, :, model + base : model + base + span]
             stacked = jnp.concatenate(
                 [jnp.where(lane_head == h, queries, 0.0).astype(jnp.bfloat16) for h in range(STACK)], axis=0
             )
@@ -295,24 +314,25 @@
             for h in range(1, STACK):
                 merged = jnp.where(lane_head == h, mean[h * QUERY_ROWS : (h + 1) * QUERY_ROWS], merged)
             attended[:, base : base + span] = merged.astype(jnp.bfloat16)
-        mixed = (embedded[rows, :].astype(jnp.float32) + dot(attended[...], pout[...])).astype(jnp.bfloat16)
+        mixed = (embedded[part, rows, :].astype(jnp.float32) + dot(attended[...], pout[...])).astype(jnp.bfloat16)
         normed = normalize(mixed, gain_two[...])
         total = mixed.astype(jnp.float32)
         for q in range(up.shape[1] // 512):
             cols = slice(q * 512, (q + 1) * 512)
             inner = gelu(dot(normed, up[:, cols])).astype(jnp.bfloat16)
             total = total + dot(inner, down[cols, :])
-        result[pl.ds(block * peers, peers)] = total.astype(jnp.bfloat16).reshape(peers, held, model)
+        first = block * peers
+        result[pl.ds(part * gap + first, peers)] = total.astype(jnp.bfloat16).reshape(peers, held, model)
         for i in range(peers):
-            peer = block * peers + i
-
-            @pl.when(peer != my_c)
+            peer = first + i
+
+            @pl.when(peer != my_lane)
             def _():
-                back(peer).start()
-
-            @pl.when(peer == my_c)
+                back(part, peer).start()
+
+            @pl.when(peer == my_lane)
             def _():
-                keep_own.start()
+                keep_own(part).start()
 
     looped(blocks, encode)
 
@@ -320,19 +340,21 @@
     looped(groups_t - 1, lambda i: hand(time_peer(i), my_t).wait_send())
 
     def finish(i):
-        peer = lax.rem(my_c + 1 + i, groups_c)
-        back(peer).wait_send()
-        pltpu.make_async_remote_copy(
-            src_ref=result.at[peer],
-            dst_ref=out.at[peer],
-            send_sem=out_send.at[peer],
-            recv_sem=out_recv.at[peer],
-            device_id=(my_t, peer),
-            device_id_type=MESH,
-        ).wait_recv()
-
-    looped(groups_c - 1, finish)
-    keep_own.wait()
+        peer = lax.rem(my_lane + 1 + i, gap)
+        for part in range(2):
+            back(part, peer).wait_send()
+            pltpu.make_async_remote_copy(
+                src_ref=result.at[part * gap + peer],
+                dst_ref=out.at[part * gap + peer],
+                send_sem=out_send.at[part * gap + peer],
+                recv_sem=out_recv.at[part * gap + peer],
+                device_id=(my_t, my_side * gap + peer),
+                device_id_type=MESH,
+            ).wait_recv()
+
+    looped(gap - 1, finish)
+    for part in range(2):
+        keep_own(part).wait()
 
 
 def per_device(
@@ -353,14 +375,15 @@
 ):
     groups_t, groups_c = lax.axis_size("tm"), lax.axis_size("chan")
     held, slab = samples.shape
-    assert slab // STRIDE == groups_c
+    assert slab // STRIDE == groups_c and groups_c % 8 == 0
     devices = groups_t * groups_c
     tokens = groups_c * held
     packs = 3 if slab * 3 <= 128 and held % 48 == 0 else 1
     model = embed_weight.shape[1]
     flat = [w.reshape(w.shape[0] * w.shape[1], w.shape[2]) for w in (dilated_one, dilated_two, dilated_three, dilated_four)]
     bf16 = jnp.bfloat16
-    width = (2 * REACH + 2) * first_kernel.shape[1]
+    gap = groups_c // 2
+    width = (2 * REACH + gap + 2) * first_kernel.shape[1]
     vmem = pl.BlockSpec(memory_space=pltpu.VMEM)
     anywhere = pl.BlockSpec(memory_space=pl.ANY)
     like = lambda w: pltpu.VMEM(w.shape, w.dtype)
@@ -377,11 +400,12 @@
             pltpu.VMEM((groups_t * slab, width), bf16),
             pltpu.VMEM((5 * dilated_one.shape[1], 2 * dilated_one.shape[2]), bf16),
             pltpu.VMEM((CONV_ROWS, width), bf16),
-            pltpu.VMEM((CONV_ROWS, 8 * 128), bf16),
-            pltpu.VMEM((CONV_ROWS, 7 * 128), bf16),
-            pltpu.VMEM((CONV_ROWS, 3 * 256), bf16),
-            pltpu.VMEM((tokens, model), bf16),
-            pltpu.VMEM((tokens, 3 * model), bf16),
+            pltpu.VMEM((CONV_ROWS, ((28 + gap) // 2 + 2) // 2 * 128), bf16),
+            pltpu.VMEM((CONV_ROWS, ((24 + gap) // 4 + 1) * 128), bf16),
+            pltpu.VMEM((CONV_ROWS, len(third_offsets(gap)) * 256), bf16),
+            pltpu.VMEM((2, tokens, model), bf16),
+            pltpu.VMEM((2, tokens, model), bf16),
+            pltpu.VMEM((2, tokens, 2 * model), bf16),
             pltpu.VMEM((QUERY_ROWS, model), bf16),
             pltpu.VMEM((groups_c, held, model), bf16),
         ]
@@ -395,7 +419,7 @@
             pltpu.SemaphoreType.DMA((groups_t,)),
             pltpu.SemaphoreType.DMA((groups_c,)),
             pltpu.SemaphoreType.DMA((groups_c,)),
-            pltpu.SemaphoreType.DMA,
+            pltpu.SemaphoreType.DMA((2,)),
         ],
         compiler_params=pltpu.CompilerParams(
             collective_id=0, has_side_effects=True, vmem_limit_bytes=56 * 2**20

time: 31.9 us -> 32.1 us (level)
  no operation moved by 1% of the time
where the time goes in v3:
time: 32.1 us; the launch traced here: 31.9 us
  Pallas kernels  30.1 us (94%)
  local copies, waits for them, and re-layouts  1.77 us (6%)
    pallas_call x1, Pallas kernels, per_device(): pl.pallas_call(functools.partial(kernel, groups_t, groups_c), out_shape=j...  30.1 us
    unnamed x1, local copies, waits for them, and re-layouts  1.77 us

profile of v3, /device:TPU:0, one launch (start us, length us, event | category | flops | bytes accessed | tf_op | source)
XLA Modules:
  0.0 31.9 jit_solution(6825973558074305632)
XLA Ops:
  0.0 30.1 %shard_map.136 = bf16[8,48,512]{2,1,0:T(8,128)(2,1)} custom-call(s32[12]{0:T(128)} %dead.1, bf16[32,48]{1,0:T(8,128)(2,1)} %bitcast.11, bf16[8,32]{1,0:T(8,128)(2,1)} %first_kernel.1, bf16[96,64]{1,0:T(8,128)(2,1)} %bitcast.10, bf16[192,128]{1,0:T(8,128)(2,1)} %bitcast.9, bf16[384,256]{1,0:T(8,128)(2,1)} %bitcast.8, bf16[768,256]{1,0:T(8,128)(2,1)} %bitcast.7, ...), custom_call_target="tpu_custom_call" | custom-call | tf_op jit(solution)/shard_map/pallas_call | solution.py:390
  30.1 1.8 %copy.16 = bf16[8,48,512]{2,1,0:T(8,128)(2,1)} copy(bf16[8,48,512]{2,1,0:T(8,128)(2,1)} %shard_map.136) | data formatting | bytes 786432
